TPU v7x, 32 devices: a whole 2x2x4 slice. The times are simulated.
32 devices in a mesh: groups: 2 (over y), expert: 16 (over z, x, core).
Axes of the slice: x: 2, y: 2, z: 4, core: 2. Of those that a mesh axis runs over, the one named last changes fastest.
Arguments:
- tokens: bfloat16 [4096, 2048], P(('groups', 'expert')), parts along dimension 0, may hold values from -6 to 6
- route_ids: int32 [4096, 8], P(('groups', 'expert')), parts along dimension 0, may hold values from 0 to 15, all different within a row; in each aligned block of 128 rows (0 to 127, 128 to 255, ...) at most 80 rows name the same one
- gates: float32 [4096, 8], P(('groups', 'expert')), parts along dimension 0, may hold values from 0.3 to 1
- w_gate: bfloat16 [16, 2048, 768], P('expert'), may hold values from -0.125 to 0.125
- w_up: bfloat16 [16, 2048, 768], P('expert'), may hold values from -0.125 to 0.125
- w_down: bfloat16 [16, 768, 2048], P('expert'), may hold values from -0.21875 to 0.21875
Outputs:
- combined: bfloat16 [4096, 2048], P(('groups', 'expert')), parts along dimension 0
There are 2 independent parts, one for each index of `groups`. A program takes and returns all parts, laid end to end along the dimension named above; an argument that names none is the same for every part. Nothing has to cross between parts.
Inputs may be any that keep to these rules, and one draw needn't show every extreme that they name: `route_ids`: each row names 8 different experts. In each aligned block of 128 rows (one device's tokens) no expert is named by more than 80 rows, a bound that some block reaches.
All inputs are finite; a program needn't handle non-finite values.
Results may differ from a plain program's by a relative error of at most 0.0058.
Values may be sent and summed in bfloat16 or wider, within the bound.
A program may use at most 128 MiB of HBM per device.

v0:
```python
import jax
import jax.numpy as jnp
from jax import lax
from jax.sharding import PartitionSpec as P


def expert_mlp(block_data, gate_local, up_local, down_local):
    gate_part = jnp.dot(block_data, gate_local, preferred_element_type=jnp.float32)
    up_part = jnp.dot(block_data, up_local, preferred_element_type=jnp.float32)
    hidden = (jax.nn.silu(gate_part) * up_part).astype(jnp.bfloat16)
    return jnp.dot(hidden, down_local, preferred_element_type=jnp.float32)


def dense_on_device(tokens, route_ids, gates, w_gate, w_up, w_down):
    n_peers = lax.axis_size("expert")
    me = lax.axis_index("expert")
    experts = jnp.arange(n_peers, dtype=jnp.int32)
    weight = jnp.sum(
        jnp.where(route_ids[:, None, :] == experts[None, :, None], gates[:, None, :], 0.0), axis=2
    )
    weights = lax.all_gather(weight, "expert", axis=0, tiled=True)
    mine = lax.dynamic_slice_in_dim(weights, me, 1, axis=1)
    everyone = lax.all_gather(tokens, "expert", axis=0, tiled=True)
    part = expert_mlp(everyone, w_gate[0], w_up[0], w_down[0])
    part = part.astype(jnp.bfloat16).astype(jnp.float32) * mine
    return lax.psum_scatter(part.astype(jnp.bfloat16), "expert", scatter_dimension=0, tiled=True)


def routed_on_device(tokens, route_ids, gates, w_gate, w_up, w_down):
    n_peers = lax.axis_size("expert")
    tok_rows, top_k = route_ids.shape
    model_width = tokens.shape[1]
    capacity = 5 * tok_rows * top_k // (4 * n_peers)
    buffer_rows = n_peers * capacity
    assigned = tok_rows * top_k
    chosen = route_ids.reshape(-1)
    onehot = (chosen[:, None] == jnp.arange(n_peers, dtype=jnp.int32)[None, :]).astype(jnp.int32)
    running = jnp.cumsum(onehot, axis=0)
    position = jnp.sum(running * onehot, axis=1) - 1
    slot_of = chosen * capacity + position
    ordinal = jnp.arange(assigned, dtype=jnp.int32)
    anchor = jnp.zeros((buffer_rows,), jnp.int32).at[slot_of].set(ordinal)
    outgoing = tokens[anchor // top_k].reshape(n_peers, capacity, model_width)
    incoming = lax.all_to_all(outgoing, "expert", split_axis=0, concat_axis=0, tiled=True)
    n_src, n_items, _ = incoming.shape
    computed = expert_mlp(
        incoming.reshape(n_src * n_items, model_width), w_gate[0], w_up[0], w_down[0]
    ).astype(jnp.bfloat16)
    computed = computed.reshape(n_src, n_items, model_width)
    returned_rows = lax.all_to_all(computed, "expert", split_axis=0, concat_axis=0, tiled=True)
    returned = returned_rows.reshape(buffer_rows, model_width)[slot_of].astype(jnp.float32)
    combined = jnp.sum(returned.reshape(tok_rows, top_k, model_width) * gates[:, :, None], axis=1)
    return combined.astype(jnp.bfloat16)


def solution(mesh):
    n_peers = mesh.shape["expert"]

    def on_device(tokens, route_ids, gates, w_gate, w_up, w_down):
        dense = n_peers <= 4 * route_ids.shape[1]
        body = dense_on_device if dense else routed_on_device
        return body(tokens, route_ids, gates, w_gate, w_up, w_down)

    in_specs = (
        P(("groups", "expert"), None),
        P(("groups", "expert"), None),
        P(("groups", "expert"), None),
        P("expert", None, None),
        P("expert", None, None),
        P("expert", None, None),
    )
    out_specs = P(("groups", "expert"), None)
    return jax.shard_map(
        on_device, mesh=mesh, in_specs=in_specs, out_specs=out_specs, check_vma=False
    )
```

profile of v0, /device:TPU:0, one launch (start us, length us, event | category | flops | bytes accessed | tf_op | source)
XLA Modules:
  0.0 228.0 jit_solution(3535841203120528709)
XLA Ops:
  6.5 0.0 copy-start
  6.5 0.0 all-gather.2.cloned.1.call-start
  6.5 0.7 all-gather.2.cloned.1.call-update
  7.3 0.0 reduce-scatter.2.cloned.1.call-start
  7.3 0.9 select_reduce_fusion
  8.2 24.1 %all_gather.7 = f32[2048,16]{0,1:T(8,128)S(1)} all-gather(f32[128,16]{0,1:T(8,128)S(1)} %select_reduce_fusion), channel_id=1, replica_groups=mesh['groups'=2,'expert'=16] {'expert'}, dimensions={0}, use_global_device_ids=true | all-gather | bytes 139264 | tf_op jit(solution)/shard_map/all_gather | solution.py:21
  32.3 54.4 %all-gather.2.cloned.1.call-done = bf16[2048,2048]{1,0:T(8,128)(2,1)} async-done(((bf16[128,2048]{1,0:T(8,128)(2,1)}), bf16[2048,2048]{1,0:T(8,128)(2,1)}) %all-gather.2.cloned.1.call-update) | async-done | bytes 8388624 | tf_op jit(solution)/shard_map/all_gather | solution.py:23
  86.7 11.7 %fusion.3 = f32[2048,768]{1,0:T(8,128)} fusion(bf16[2048,2048]{1,0:T(8,128)(2,1)} %all-gather.2.cloned.1.call-done, bf16[1,2048,768]{2,1,0:T(8,128)(2,1)} %param.9), kind=kOutput, calls=%fused_computation.4 | convolution fusion | flops 6442450944 | bytes 17825792 | tf_op jit(solution)/shard_map/dot_general | solution.py:8
  98.4 0.0 copy-done
  98.4 20.6 %multiply_convert_fusion = bf16[2048,2048]{1,0:T(8,128)(2,1)} fusion(f32[2048]{0:T(1024)S(1)} %bitcast.13, f32[2048,768]{1,0:T(8,128)} %fusion.3, bf16[2048,2048]{1,0:T(8,128)(2,1)} %all-gather.2.cloned.1.call-done, bf16[1,768,2048]{2,1,0:T(8,128)(2,1)S(1)} %copy-done, bf16[1,2048,768]{2,1,0:T(8,128)(2,1)} %param.10), kind=kOutput, calls=%fused_computation | convolution fusion | flops 12911116288 | bytes 29368320 | tf_op jit(solution)/shard_map/dot_general | solution.py:11
  119.0 0.0 reduce-scatter.2.cloned.1.call-update
  119.0 102.2 %reduce-scatter.2.cloned.1.call-done = bf16[128,2048]{1,0:T(8,128)(2,1)} async-done(((bf16[2048,2048]{1,0:T(8,128)(2,1)}), bf16[128,2048]{1,0:T(8,128)(2,1)}) %reduce-scatter.2.cloned.1.call-update) | async-done | bytes 524304 | tf_op jit(solution)/shard_map/reduce_scatter | solution.py:26
  (1 shorter events, 0.0 us)
Async XLA Ops:
  6.5 91.9 %copy-start = (bf16[1,768,2048]{2,1,0:T(8,128)(2,1)S(1)}, bf16[1,768,2048]{2,1,0:T(8,128)(2,1)}, u32[]{:S(2)}) copy-start(bf16[1,768,2048]{2,1,0:T(8,128)(2,1)} %param.11) | copy-start | bytes 9437188
  6.5 80.2 %all-gather.2.cloned.1.call-start = ((), (), s32[]{:S(2)}) async-start(), calls=%async_computation.1 | async-start | bytes 8912896 | tf_op jit(solution)/shard_map/all_gather | solution.py:23
  7.3 213.9 %reduce-scatter.2.cloned.1.call-start = ((), (), s32[]{:S(2)}) async-start(), calls=%async_computation.2 | async-start | bytes 8912896 | tf_op jit(solution)/shard_map/reduce_scatter | solution.py:26
Sparse Core Ops, SparseCore 0:
  9.5 77.1 all-gather.1
  119.1 102.0 reduce-scatter.1
where the time goes:
time: 228 us
  waiting for transfers between devices  157 us (69%)
  matrix products  32.3 us (14%)
  blocking collectives  24.1 us (11%)
  between operations  13.4 us (6%)
    reduce_scatter x1, waiting for transfers between devices, dense_on_device(): lax.psum_scatter(part.astype(jnp.bfloat16), 'expert', scatter_dimension=0...  102 us
    all_gather x1, waiting for transfers between devices, dense_on_device(): everyone = lax.all_gather(tokens, 'expert', axis=0, tiled=True)  54.4 us
    all_gather x1, blocking collectives, dense_on_device(): weights = lax.all_gather(weight, 'expert', axis=0, tiled=True)  24.1 us
    dot_general x1, matrix products, expert_mlp(): return jnp.dot(hidden, down_local, preferred_element_type=jnp.float32)  20.6 us
    dot_general x1, matrix products, expert_mlp(): jnp.dot(block_data, gate_local, preferred_element_type=jnp.float32)  11.7 us
  transfers between devices with their start and end apart: 2, of which 2 were waited for; matrix products, arithmetic and copies ran while one was open for 0% of the time, Pallas kernels for 0%

commit v1 on v0

--- a/solution.py
+++ b/solution.py
@@ -20,7 +20,14 @@
     )
     weights = lax.all_gather(weight, "expert", axis=0, tiled=True)
     mine = lax.dynamic_slice_in_dim(weights, me, 1, axis=1)
-    everyone = lax.all_gather(tokens, "expert", axis=0, tiled=True)
+    ring = [tokens]
+    for hop in range(15):
+        ring.append(lax.ppermute(ring[-1], "expert", [(dev, (dev + 1) % 16) for dev in range(16)]))
+    everyone = jnp.roll(
+        jnp.concatenate(ring[::-1], axis=0),
+        (lax.axis_index("expert") + 1) * ring[0].shape[0],
+        axis=0,
+    )
     part = expert_mlp(everyone, w_gate[0], w_up[0], w_down[0])
     part = part.astype(jnp.bfloat16).astype(jnp.float32) * mine
     return lax.psum_scatter(part.astype(jnp.bfloat16), "expert", scatter_dimension=0, tiled=True)

time: 228 us -> 357 us (1.57)
  waiting for transfers between devices: 157 us -> 260 us
  local copies, waits for them, and re-layouts: 0.01 us -> 30.6 us
  blocking collectives: 24.1 us -> 20.4 us
    ppermute x0 -> x15, waiting for transfers between devices: none -> 159 us  [dense_on_device(): lax.ppermute(ring[-1], 'expert', [(dev, (dev + 1) % 16) for dev in range(...]
    all_gather x1 -> x0, waiting for transfers between devices: 54.4 us -> none  [dense_on_device(): everyone = lax.all_gather(tokens, 'expert', axis=0, tiled=True)]
    unnamed x2 -> x91, local copies, waits for them, and re-layouts: 0.01 us -> 30.5 us
    all_gather x1, blocking collectives: 24.1 us -> 20.4 us  [dense_on_device(): weights = lax.all_gather(weight, 'expert', axis=0, tiled=True)]
  transfers between devices with their start and end apart: 2 -> 16, of which waited for: 2 -> 15; matrix products, arithmetic and copies ran while one was open for 0% -> 0% of each run, Pallas kernels for 0% -> 0%
where the time goes in v1:
time: 357 us; the launch traced here: 356 us
  waiting for transfers between devices  260 us (73%)
  local copies, waits for them, and re-layouts  30.6 us (9%)
  matrix products  29.3 us (8%)
  blocking collectives  20.4 us (6%)
  between operations  13.8 us (4%)
    ppermute x15, waiting for transfers between devices, dense_on_device(): lax.ppermute(ring[-1], 'expert', [(dev, (dev + 1) % 16) for dev in range(...  159 us
    reduce_scatter x1, waiting for transfers between devices, dense_on_device(): lax.psum_scatter(part.astype(jnp.bfloat16), 'expert', scatter_dimension=0...  101 us
    unnamed x91, local copies, waits for them, and re-layouts  30.5 us
    dot_general x1, matrix products, expert_mlp(): return jnp.dot(hidden, down_local, preferred_element_type=jnp.float32)  20.8 us
    all_gather x1, blocking collectives, dense_on_device(): weights = lax.all_gather(weight, 'expert', axis=0, tiled=True)  20.4 us
    dot_general x1, matrix products, expert_mlp(): up_part = jnp.dot(block_data, up_local, preferred_element_type=jnp.float32)  8.56 us
  transfers between devices with their start and end apart: 16, of which 15 were waited for; matrix products, arithmetic and copies ran while one was open for 0% of the time, Pallas kernels for 0%

profile of v1, /device:TPU:0, one launch (start us, length us, event | category | flops | bytes accessed | tf_op | source)
XLA Modules:
  0.0 356.0 jit_solution(13927726400886991720)
XLA Ops:
  6.5 0.5 collective-permute-start
  7.0 12.0 %collective-permute-done = bf16[128,2048]{1,0:T(8,128)(2,1)S(1)} collective-permute-done((bf16[128,2048]{1,0:T(8,128)(2,1)}, bf16[128,2048]{1,0:T(8,128)(2,1)S(1)}, u32[]{:S(2)}, u32[]{:S(2)}) %collective-permute-start) | collective-permute-done | bytes 524320 | tf_op jit(solution)/shard_map/ppermute | solution.py:25
  19.1 0.8 copy-done.2
  19.8 0.0 collective-permute-start.1
  19.8 11.3 %collective-permute-done.1 = bf16[128,2048]{1,0:T(8,128)(2,1)S(1)} collective-permute-done((bf16[128,2048]{1,0:T(8,128)(2,1)S(1)}, bf16[128,2048]{1,0:T(8,128)(2,1)S(1)}, u32[]{:S(2)}, u32[]{:S(2)}) %collective-permute-start.1) | collective-permute-done | bytes 524320 | tf_op jit(solution)/shard_map/ppermute | solution.py:25
  31.1 0.8 copy-done.4
  32.0 0.0 collective-permute-start.2
  32.0 11.3 %collective-permute-done.2 = bf16[128,2048]{1,0:T(8,128)(2,1)S(1)} collective-permute-done((bf16[128,2048]{1,0:T(8,128)(2,1)S(1)}, bf16[128,2048]{1,0:T(8,128)(2,1)S(1)}, u32[]{:S(2)}, u32[]{:S(2)}) %collective-permute-start.2) | collective-permute-done | bytes 524320 | tf_op jit(solution)/shard_map/ppermute | solution.py:25
  43.3 0.8 copy-done.6
  44.1 0.0 collective-permute-start.3
  44.1 11.3 %collective-permute-done.3 = bf16[128,2048]{1,0:T(8,128)(2,1)S(1)} collective-permute-done((bf16[128,2048]{1,0:T(8,128)(2,1)S(1)}, bf16[128,2048]{1,0:T(8,128)(2,1)S(1)}, u32[]{:S(2)}, u32[]{:S(2)}) %collective-permute-start.3) | collective-permute-done | bytes 524320 | tf_op jit(solution)/shard_map/ppermute | solution.py:25
  55.4 0.8 copy-done.8
  56.2 0.0 collective-permute-start.4
  56.2 11.3 %collective-permute-done.4 = bf16[128,2048]{1,0:T(8,128)(2,1)S(1)} collective-permute-done((bf16[128,2048]{1,0:T(8,128)(2,1)S(1)}, bf16[128,2048]{1,0:T(8,128)(2,1)S(1)}, u32[]{:S(2)}, u32[]{:S(2)}) %collective-permute-start.4) | collective-permute-done | bytes 524320 | tf_op jit(solution)/shard_map/ppermute | solution.py:25
  67.5 0.8 copy-done.10
  68.3 0.0 collective-permute-start.5
  68.3 11.3 %collective-permute-done.5 = bf16[128,2048]{1,0:T(8,128)(2,1)S(1)} collective-permute-done((bf16[128,2048]{1,0:T(8,128)(2,1)S(1)}, bf16[128,2048]{1,0:T(8,128)(2,1)S(1)}, u32[]{:S(2)}, u32[]{:S(2)}) %collective-permute-start.5) | collective-permute-done | bytes 524320 | tf_op jit(solution)/shard_map/ppermute | solution.py:25
  79.6 0.8 copy-done.12
  80.4 11.3 %collective-permute-done.6 = bf16[128,2048]{1,0:T(8,128)(2,1)S(1)} collective-permute-done((bf16[128,2048]{1,0:T(8,128)(2,1)S(1)}, bf16[128,2048]{1,0:T(8,128)(2,1)S(1)}, u32[]{:S(2)}, u32[]{:S(2)}) %collective-permute-start.6) | collective-permute-done | bytes 524320 | tf_op jit(solution)/shard_map/ppermute | solution.py:25
  91.7 0.8 copy-done.14
  92.5 0.0 collective-permute-start.7
  92.5 11.3 %collective-permute-done.7 = bf16[128,2048]{1,0:T(8,128)(2,1)S(1)} collective-permute-done((bf16[128,2048]{1,0:T(8,128)(2,1)S(1)}, bf16[128,2048]{1,0:T(8,128)(2,1)S(1)}, u32[]{:S(2)}, u32[]{:S(2)}) %collective-permute-start.7) | collective-permute-done | bytes 524320 | tf_op jit(solution)/shard_map/ppermute | solution.py:25
  103.8 0.8 copy-done.16
  104.6 0.0 collective-permute-start.8
  104.6 11.3 %collective-permute-done.8 = bf16[128,2048]{1,0:T(8,128)(2,1)S(1)} collective-permute-done((bf16[128,2048]{1,0:T(8,128)(2,1)S(1)}, bf16[128,2048]{1,0:T(8,128)(2,1)S(1)}, u32[]{:S(2)}, u32[]{:S(2)}) %collective-permute-start.8) | collective-permute-done | bytes 524320 | tf_op jit(solution)/shard_map/ppermute | solution.py:25
  115.9 0.8 copy-done.18
  116.7 11.3 %collective-permute-done.9 = bf16[128,2048]{1,0:T(8,128)(2,1)S(1)} collective-permute-done((bf16[128,2048]{1,0:T(8,128)(2,1)S(1)}, bf16[128,2048]{1,0:T(8,128)(2,1)S(1)}, u32[]{:S(2)}, u32[]{:S(2)}) %collective-permute-start.9) | collective-permute-done | bytes 524320 | tf_op jit(solution)/shard_map/ppermute | solution.py:25
  128.0 0.8 copy-done.20
  128.9 11.3 %collective-permute-done.10 = bf16[128,2048]{1,0:T(8,128)(2,1)S(1)} collective-permute-done((bf16[128,2048]{1,0:T(8,128)(2,1)S(1)}, bf16[128,2048]{1,0:T(8,128)(2,1)S(1)}, u32[]{:S(2)}, u32[]{:S(2)}) %collective-permute-start.10) | collective-permute-done | bytes 524320 | tf_op jit(solution)/shard_map/ppermute | solution.py:25
  140.2 0.8 copy-done.22
  141.0 11.3 %collective-permute-done.11 = bf16[128,2048]{1,0:T(8,128)(2,1)S(1)} collective-permute-done((bf16[128,2048]{1,0:T(8,128)(2,1)S(1)}, bf16[128,2048]{1,0:T(8,128)(2,1)S(1)}, u32[]{:S(2)}, u32[]{:S(2)}) %collective-permute-start.11) | collective-permute-done | bytes 524320 | tf_op jit(solution)/shard_map/ppermute | solution.py:25
  152.3 0.8 copy-done.24
  153.1 0.0 collective-permute-start.12
  153.1 11.3 %collective-permute-done.12 = bf16[128,2048]{1,0:T(8,128)(2,1)S(1)} collective-permute-done((bf16[128,2048]{1,0:T(8,128)(2,1)S(1)}, bf16[128,2048]{1,0:T(8,128)(2,1)S(1)}, u32[]{:S(2)}, u32[]{:S(2)}) %collective-permute-start.12) | collective-permute-done | bytes 524320 | tf_op jit(solution)/shard_map/ppermute | solution.py:25
  164.4 0.8 copy-done.26
  165.2 11.5 %collective-permute-done.13 = bf16[128,2048]{1,0:T(8,128)(2,1)} collective-permute-done((bf16[128,2048]{1,0:T(8,128)(2,1)S(1)}, bf16[128,2048]{1,0:T(8,128)(2,1)}, u32[]{:S(2)}, u32[]{:S(2)}) %collective-permute-start.13) | collective-permute-done | bytes 524320 | tf_op jit(solution)/shard_map/ppermute | solution.py:25
  176.7 0.0 collective-permute-start.14
  176.8 0.0 copy-start.1
  176.8 0.9 select_reduce_fusion
  177.7 20.4 %all_gather.3 = f32[2048,16]{0,1:T(8,128)S(1)} all-gather(f32[128,16]{0,1:T(8,128)S(1)} %select_reduce_fusion), channel_id=1, replica_groups=mesh['groups'=2,'expert'=16] {'expert'}, dimensions={0}, use_global_device_ids=true | all-gather | bytes 139264 | tf_op jit(solution)/shard_map/all_gather | solution.py:21
  198.1 0.0 copy-start.29
  198.1 0.0 collective-permute-done.14
  198.1 1.2 constant_dynamic-update-slice_fusion.31
  199.3 1.1 constant_dynamic-update-slice_fusion.30
  200.4 1.1 constant_dynamic-update-slice_fusion.29
  201.5 1.1 constant_dynamic-update-slice_fusion.28
  202.6 1.1 constant_dynamic-update-slice_fusion.27
  203.7 1.1 constant_dynamic-update-slice_fusion.26
  204.7 1.1 constant_dynamic-update-slice_fusion.25
  205.8 1.1 constant_dynamic-update-slice_fusion.24
  206.9 1.1 constant_dynamic-update-slice_fusion.23
  208.0 1.1 constant_dynamic-update-slice_fusion.22
  209.1 1.1 constant_dynamic-update-slice_fusion.21
  210.1 1.1 constant_dynamic-update-slice_fusion.20
  211.2 1.1 constant_dynamic-update-slice_fusion.19
  212.3 1.1 constant_dynamic-update-slice_fusion.18
  213.4 1.1 constant_dynamic-update-slice_fusion.17
  214.5 1.1 constant_dynamic-update-slice_fusion.16
  215.6 1.1 constant_dynamic-update-slice_fusion.15
  216.6 1.1 constant_dynamic-update-slice_fusion.14
  218.5 8.6 %fusion = f32[2048,768]{1,0:T(8,128)} fusion(bf16[4096,2048]{1,0:T(8,128)(2,1)S(1)} %constant_dynamic-update-slice_fusion, s32[]{:T(128)S(6)} %select_n.21, bf16[1,2048,768]{2,1,0:T(8,128)(2,1)S(1)} %copy-done.29), kind=kOutput, calls=%fused_computation.1 | convolution fusion | flops 6442450944 | bytes 17825796 | tf_op jit(solution)/shard_map/dot_general | solution.py:9
  227.1 20.8 %multiply_convert_fusion = bf16[2048,2048]{1,0:T(8,128)(2,1)} fusion(f32[2048]{0:T(1024)S(1)} %bitcast.11, f32[2048,768]{1,0:T(8,128)} %fusion, bf16[4096,2048]{1,0:T(8,128)(2,1)} %copy-done.28, s32[]{:T(128)S(6)} %select_n.21, bf16[1,768,2048]{2,1,0:T(8,128)(2,1)S(1)} %copy-done, bf16[1,2048,768]{2,1,0:T(8,128)(2,1)} %param.9), kind=kOutput, calls=%fused_computation | convolution fusion | flops 12911116288 | bytes 29368324 | tf_op jit(solution)/shard_map/dot_general | solution.py:11
  247.8 0.0 reduce-scatter.2.cloned.1.call-update
  247.8 101.3 %reduce-scatter.2.cloned.1.call-done = bf16[128,2048]{1,0:T(8,128)(2,1)} async-done(((bf16[2048,2048]{1,0:T(8,128)(2,1)}), bf16[128,2048]{1,0:T(8,128)(2,1)}) %reduce-scatter.2.cloned.1.call-update) | async-done | bytes 524304 | tf_op jit(solution)/shard_map/reduce_scatter | solution.py:33
  (66 shorter events, 0.6 us)
Async XLA Ops:
  6.5 220.5 %copy-start = (bf16[1,768,2048]{2,1,0:T(8,128)(2,1)S(1)}, bf16[1,768,2048]{2,1,0:T(8,128)(2,1)}, u32[]{:S(2)}) copy-start(bf16[1,768,2048]{2,1,0:T(8,128)(2,1)} %param.11) | copy-start | bytes 9437188
  6.5 342.6 %reduce-scatter.2.cloned.1.call-start = ((), (), s32[]{:S(2)}) async-start(), calls=%async_computation.1 | async-start | bytes 8912896 | tf_op jit(solution)/shard_map/reduce_scatter | solution.py:33
  6.5 12.5 %collective-permute-start = (bf16[128,2048]{1,0:T(8,128)(2,1)}, bf16[128,2048]{1,0:T(8,128)(2,1)S(1)}, u32[]{:S(2)}, u32[]{:S(2)}) collective-permute-start(bf16[128,2048]{1,0:T(8,128)(2,1)} %param.6), channel_id=1, source_target_pairs={{0,1},{1,2},{2,3},{3,4},{4,5},{5,6},{6,7},{7,8},{8,9},{9,10},{10,1... | collective-permute-start | bytes 1572872 | tf_op jit(solution)/shard_map/ppermute | solution.py:25
  19.1 0.8 copy-start.2
  19.8 11.3 %collective-permute-start.1 = (bf16[128,2048]{1,0:T(8,128)(2,1)S(1)}, bf16[128,2048]{1,0:T(8,128)(2,1)S(1)}, u32[]{:S(2)}, u32[]{:S(2)}) collective-permute-start(bf16[128,2048]{1,0:T(8,128)(2,1)S(1)} %collective-permute-done), channel_id=1, source_target_pairs={{0,1},{1,2},{2,3},{3,4},{4,5},{5,6},{6,7},{7,8},{8,9},{9,10},{10,1... | collective-permute-start | bytes 1572872 | tf_op jit(solution)/shard_map/ppermute | solution.py:25
  31.1 0.8 copy-start.4
  32.0 11.3 %collective-permute-start.2 = (bf16[128,2048]{1,0:T(8,128)(2,1)S(1)}, bf16[128,2048]{1,0:T(8,128)(2,1)S(1)}, u32[]{:S(2)}, u32[]{:S(2)}) collective-permute-start(bf16[128,2048]{1,0:T(8,128)(2,1)S(1)} %collective-permute-done.1), channel_id=1, source_target_pairs={{0,1},{1,2},{2,3},{3,4},{4,5},{5,6},{6,7},{7,8},{8,9},{9,10},{10,1... | collective-permute-start | bytes 1572872 | tf_op jit(solution)/shard_map/ppermute | solution.py:25
  43.3 0.8 copy-start.6
  44.1 11.3 %collective-permute-start.3 = (bf16[128,2048]{1,0:T(8,128)(2,1)S(1)}, bf16[128,2048]{1,0:T(8,128)(2,1)S(1)}, u32[]{:S(2)}, u32[]{:S(2)}) collective-permute-start(bf16[128,2048]{1,0:T(8,128)(2,1)S(1)} %collective-permute-done.2), channel_id=1, source_target_pairs={{0,1},{1,2},{2,3},{3,4},{4,5},{5,6},{6,7},{7,8},{8,9},{9,10},{10,1... | collective-permute-start | bytes 1572872 | tf_op jit(solution)/shard_map/ppermute | solution.py:25
  55.4 0.8 copy-start.8
  56.2 11.3 %collective-permute-start.4 = (bf16[128,2048]{1,0:T(8,128)(2,1)S(1)}, bf16[128,2048]{1,0:T(8,128)(2,1)S(1)}, u32[]{:S(2)}, u32[]{:S(2)}) collective-permute-start(bf16[128,2048]{1,0:T(8,128)(2,1)S(1)} %collective-permute-done.3), channel_id=1, source_target_pairs={{0,1},{1,2},{2,3},{3,4},{4,5},{5,6},{6,7},{7,8},{8,9},{9,10},{10,1... | collective-permute-start | bytes 1572872 | tf_op jit(solution)/shard_map/ppermute | solution.py:25
  67.5 0.8 copy-start.10
  68.3 11.3 %collective-permute-start.5 = (bf16[128,2048]{1,0:T(8,128)(2,1)S(1)}, bf16[128,2048]{1,0:T(8,128)(2,1)S(1)}, u32[]{:S(2)}, u32[]{:S(2)}) collective-permute-start(bf16[128,2048]{1,0:T(8,128)(2,1)S(1)} %collective-permute-done.4), channel_id=1, source_target_pairs={{0,1},{1,2},{2,3},{3,4},{4,5},{5,6},{6,7},{7,8},{8,9},{9,10},{10,1... | collective-permute-start | bytes 1572872 | tf_op jit(solution)/shard_map/ppermute | solution.py:25
  79.6 0.8 copy-start.12
  80.4 11.3 %collective-permute-start.6 = (bf16[128,2048]{1,0:T(8,128)(2,1)S(1)}, bf16[128,2048]{1,0:T(8,128)(2,1)S(1)}, u32[]{:S(2)}, u32[]{:S(2)}) collective-permute-start(bf16[128,2048]{1,0:T(8,128)(2,1)S(1)} %collective-permute-done.5), channel_id=1, source_target_pairs={{0,1},{1,2},{2,3},{3,4},{4,5},{5,6},{6,7},{7,8},{8,9},{9,10},{10,1... | collective-permute-start | bytes 1572872 | tf_op jit(solution)/shard_map/ppermute | solution.py:25
  91.7 0.8 copy-start.14
  92.5 11.3 %collective-permute-start.7 = (bf16[128,2048]{1,0:T(8,128)(2,1)S(1)}, bf16[128,2048]{1,0:T(8,128)(2,1)S(1)}, u32[]{:S(2)}, u32[]{:S(2)}) collective-permute-start(bf16[128,2048]{1,0:T(8,128)(2,1)S(1)} %collective-permute-done.6), channel_id=1, source_target_pairs={{0,1},{1,2},{2,3},{3,4},{4,5},{5,6},{6,7},{7,8},{8,9},{9,10},{10,1... | collective-permute-start | bytes 1572872 | tf_op jit(solution)/shard_map/ppermute | solution.py:25
  103.8 0.8 copy-start.16
  104.6 11.3 %collective-permute-start.8 = (bf16[128,2048]{1,0:T(8,128)(2,1)S(1)}, bf16[128,2048]{1,0:T(8,128)(2,1)S(1)}, u32[]{:S(2)}, u32[]{:S(2)}) collective-permute-start(bf16[128,2048]{1,0:T(8,128)(2,1)S(1)} %collective-permute-done.7), channel_id=1, source_target_pairs={{0,1},{1,2},{2,3},{3,4},{4,5},{5,6},{6,7},{7,8},{8,9},{9,10},{10,1... | collective-permute-start | bytes 1572872 | tf_op jit(solution)/shard_map/ppermute | solution.py:25
  115.9 0.8 copy-start.18
  116.7 11.3 %collective-permute-start.9 = (bf16[128,2048]{1,0:T(8,128)(2,1)S(1)}, bf16[128,2048]{1,0:T(8,128)(2,1)S(1)}, u32[]{:S(2)}, u32[]{:S(2)}) collective-permute-start(bf16[128,2048]{1,0:T(8,128)(2,1)S(1)} %collective-permute-done.8), channel_id=1, source_target_pairs={{0,1},{1,2},{2,3},{3,4},{4,5},{5,6},{6,7},{7,8},{8,9},{9,10},{10,1... | collective-permute-start | bytes 1572872 | tf_op jit(solution)/shard_map/ppermute | solution.py:25
  128.0 0.8 copy-start.20
  128.8 11.3 %collective-permute-start.10 = (bf16[128,2048]{1,0:T(8,128)(2,1)S(1)}, bf16[128,2048]{1,0:T(8,128)(2,1)S(1)}, u32[]{:S(2)}, u32[]{:S(2)}) collective-permute-start(bf16[128,2048]{1,0:T(8,128)(2,1)S(1)} %collective-permute-done.9), channel_id=1, source_target_pairs={{0,1},{1,2},{2,3},{3,4},{4,5},{5,6},{6,7},{7,8},{8,9},{9,10},{10,1... | collective-permute-start | bytes 1572872 | tf_op jit(solution)/shard_map/ppermute | solution.py:25
  140.2 0.8 copy-start.22
  140.9 11.3 %collective-permute-start.11 = (bf16[128,2048]{1,0:T(8,128)(2,1)S(1)}, bf16[128,2048]{1,0:T(8,128)(2,1)S(1)}, u32[]{:S(2)}, u32[]{:S(2)}) collective-permute-start(bf16[128,2048]{1,0:T(8,128)(2,1)S(1)} %collective-permute-done.10), channel_id=1, source_target_pairs={{0,1},{1,2},{2,3},{3,4},{4,5},{5,6},{6,7},{7,8},{8,9},{9,10},{10,1... | collective-permute-start | bytes 1572872 | tf_op jit(solution)/shard_map/ppermute | solution.py:25
  152.3 0.8 copy-start.24
  153.1 11.3 %collective-permute-start.12 = (bf16[128,2048]{1,0:T(8,128)(2,1)S(1)}, bf16[128,2048]{1,0:T(8,128)(2,1)S(1)}, u32[]{:S(2)}, u32[]{:S(2)}) collective-permute-start(bf16[128,2048]{1,0:T(8,128)(2,1)S(1)} %collective-permute-done.11), channel_id=1, source_target_pairs={{0,1},{1,2},{2,3},{3,4},{4,5},{5,6},{6,7},{7,8},{8,9},{9,10},{10,1... | collective-permute-start | bytes 1572872 | tf_op jit(solution)/shard_map/ppermute | solution.py:25
  164.4 0.8 copy-start.26
  165.2 11.5 %collective-permute-start.13 = (bf16[128,2048]{1,0:T(8,128)(2,1)S(1)}, bf16[128,2048]{1,0:T(8,128)(2,1)}, u32[]{:S(2)}, u32[]{:S(2)}) collective-permute-start(bf16[128,2048]{1,0:T(8,128)(2,1)S(1)} %collective-permute-done.12), channel_id=1, source_target_pairs={{0,1},{1,2},{2,3},{3,4},{4,5},{5,6},{6,7},{7,8},{8,9},{9,10},{10,1... | collective-permute-start | bytes 1572872 | tf_op jit(solution)/shard_map/ppermute | solution.py:25
  176.7 21.4 %collective-permute-start.14 = (bf16[128,2048]{1,0:T(8,128)(2,1)}, bf16[128,2048]{1,0:T(8,128)(2,1)}, u32[]{:S(2)}, u32[]{:S(2)}) collective-permute-start(bf16[128,2048]{1,0:T(8,128)(2,1)} %collective-permute-done.13), channel_id=1, source_target_pairs={{0,1},{1,2},{2,3},{3,4},{4,5},{5,6},{6,7},{7,8},{8,9},{9,10},{10,1... | collective-permute-start | bytes 1572872 | tf_op jit(solution)/shard_map/ppermute | solution.py:25
  176.7 41.0 %copy-start.27 = (bf16[128,2048]{1,0:T(8,128)(2,1)S(1)}, bf16[128,2048]{1,0:T(8,128)(2,1)}, u32[]{:S(2)}) copy-start(bf16[128,2048]{1,0:T(8,128)(2,1)} %copy-done.26) | copy-start | bytes 1572868
  176.7 41.1 %copy-start.25 = (bf16[128,2048]{1,0:T(8,128)(2,1)S(1)}, bf16[128,2048]{1,0:T(8,128)(2,1)}, u32[]{:S(2)}) copy-start(bf16[128,2048]{1,0:T(8,128)(2,1)} %copy-done.24) | copy-start | bytes 1572868
  176.7 41.2 %copy-start.23 = (bf16[128,2048]{1,0:T(8,128)(2,1)S(1)}, bf16[128,2048]{1,0:T(8,128)(2,1)}, u32[]{:S(2)}) copy-start(bf16[128,2048]{1,0:T(8,128)(2,1)} %copy-done.22) | copy-start | bytes 1572868
  176.7 41.2 %copy-start.21 = (bf16[128,2048]{1,0:T(8,128)(2,1)S(1)}, bf16[128,2048]{1,0:T(8,128)(2,1)}, u32[]{:S(2)}) copy-start(bf16[128,2048]{1,0:T(8,128)(2,1)} %copy-done.20) | copy-start | bytes 1572868
  176.7 41.2 %copy-start.19 = (bf16[128,2048]{1,0:T(8,128)(2,1)S(1)}, bf16[128,2048]{1,0:T(8,128)(2,1)}, u32[]{:S(2)}) copy-start(bf16[128,2048]{1,0:T(8,128)(2,1)} %copy-done.18) | copy-start | bytes 1572868
  176.7 41.3 %copy-start.17 = (bf16[128,2048]{1,0:T(8,128)(2,1)S(1)}, bf16[128,2048]{1,0:T(8,128)(2,1)}, u32[]{:S(2)}) copy-start(bf16[128,2048]{1,0:T(8,128)(2,1)} %copy-done.16) | copy-start | bytes 1572868
  176.7 41.3 %copy-start.15 = (bf16[128,2048]{1,0:T(8,128)(2,1)S(1)}, bf16[128,2048]{1,0:T(8,128)(2,1)}, u32[]{:S(2)}) copy-start(bf16[128,2048]{1,0:T(8,128)(2,1)} %copy-done.14) | copy-start | bytes 1572868
  176.7 41.4 %copy-start.13 = (bf16[128,2048]{1,0:T(8,128)(2,1)S(1)}, bf16[128,2048]{1,0:T(8,128)(2,1)}, u32[]{:S(2)}) copy-start(bf16[128,2048]{1,0:T(8,128)(2,1)} %copy-done.12) | copy-start | bytes 1572868
  176.7 41.4 %copy-start.11 = (bf16[128,2048]{1,0:T(8,128)(2,1)S(1)}, bf16[128,2048]{1,0:T(8,128)(2,1)}, u32[]{:S(2)}) copy-start(bf16[128,2048]{1,0:T(8,128)(2,1)} %copy-done.10) | copy-start | bytes 1572868
  176.7 41.5 %copy-start.9 = (bf16[128,2048]{1,0:T(8,128)(2,1)S(1)}, bf16[128,2048]{1,0:T(8,128)(2,1)}, u32[]{:S(2)}) copy-start(bf16[128,2048]{1,0:T(8,128)(2,1)} %copy-done.8) | copy-start | bytes 1572868
  176.7 41.5 %copy-start.7 = (bf16[128,2048]{1,0:T(8,128)(2,1)S(1)}, bf16[128,2048]{1,0:T(8,128)(2,1)}, u32[]{:S(2)}) copy-start(bf16[128,2048]{1,0:T(8,128)(2,1)} %copy-done.6) | copy-start | bytes 1572868
  176.8 41.6 %copy-start.5 = (bf16[128,2048]{1,0:T(8,128)(2,1)S(1)}, bf16[128,2048]{1,0:T(8,128)(2,1)}, u32[]{:S(2)}) copy-start(bf16[128,2048]{1,0:T(8,128)(2,1)} %copy-done.4) | copy-start | bytes 1572868
  176.8 41.6 %copy-start.3 = (bf16[128,2048]{1,0:T(8,128)(2,1)S(1)}, bf16[128,2048]{1,0:T(8,128)(2,1)}, u32[]{:S(2)}) copy-start(bf16[128,2048]{1,0:T(8,128)(2,1)} %copy-done.2) | copy-start | bytes 1572868
  176.8 41.6 %copy-start.1 = (bf16[128,2048]{1,0:T(8,128)(2,1)S(1)}, bf16[128,2048]{1,0:T(8,128)(2,1)}, u32[]{:S(2)}) copy-start(bf16[128,2048]{1,0:T(8,128)(2,1)} %param.6) | copy-start | bytes 1572868
  198.1 20.4 %copy-start.29 = (bf16[1,2048,768]{2,1,0:T(8,128)(2,1)S(1)}, bf16[1,2048,768]{2,1,0:T(8,128)(2,1)}, u32[]{:S(2)}) copy-start(bf16[1,2048,768]{2,1,0:T(8,128)(2,1)} %param.10) | copy-start | bytes 9437188
  218.5 8.6 %copy-start.28 = (bf16[4096,2048]{1,0:T(8,128)(2,1)}, bf16[4096,2048]{1,0:T(8,128)(2,1)S(1)}, u32[]{:S(2)}) copy-start(bf16[4096,2048]{1,0:T(8,128)(2,1)S(1)} %constant_dynamic-update-slice_fusion) | copy-start | bytes 50331652
Sparse Core Ops, SparseCore 0:
  248.0 101.1 reduce-scatter.1
